TPU v7x, 256 devices: a whole 4x4x8 slice. The times are simulated.
256 devices in a mesh: pair: 64 (over x, z, core), virt: 4 (over y).
Axes of the slice: x: 4, y: 4, z: 8, core: 2. Of those that a mesh axis runs over, the one named last changes fastest.
Arguments:
- amplitudes: bfloat16 [65536, 8, 1024], P('pair', 'virt'), may hold values from -6 to 6
- tile_mask: int32 [65536, 8], P('pair', 'virt'), may hold values from 0 to 1
- integrals: bfloat16 [8, 1024, 1024], P('virt', 'pair'), may hold values from -0.0625 to 0.0625
- pair_energy: float32 [65536], P(('pair', 'virt')), may hold values from -2 to -0.5
- virt_energy: float32 [1024], replicated, may hold values from 0.5 to 3
Outputs:
- update: bfloat16 [65536, 1024], P(('pair', 'virt'))
All inputs are finite; a program needn't handle non-finite values.
Results may differ from a plain program's by a relative error of at most 0.011.
Values may be sent and summed in bfloat16 or wider, within the bound.
A program may use at most 64 MiB of HBM per device.

v0:
```python
import jax
import jax.numpy as jnp
from jax import lax
from jax.sharding import PartitionSpec as P


def on_device(amplitudes, tile_mask, integrals, pair_energy, virt_energy):
    masked = amplitudes * tile_mask.astype(jnp.bfloat16)[:, :, None]
    partial_value = jnp.einsum(
        "ptk,tkn->pn",
        masked,
        lax.all_gather(integrals, "pair", axis=1, tiled=True),
        preferred_element_type=jnp.float32,
    )
    ladder = lax.psum_scatter(
        partial_value.astype(jnp.bfloat16), "virt", scatter_dimension=0, tiled=True
    ).astype(jnp.float32)
    denom = virt_energy[None, :] - pair_energy[:, None]
    return (ladder / denom).astype(jnp.bfloat16)


def solution(mesh):
    placed = (
        P("pair", "virt", None),
        P("pair", "virt"),
        P("virt", "pair", None),
        P(("pair", "virt")),
        P(),
    )
    return jax.shard_map(
        on_device, mesh=mesh, in_specs=placed, out_specs=P(("pair", "virt"), None), check_vma=False
    )
```

profile of v0, /device:TPU:1, one launch (start us, length us, event | category | flops | bytes accessed | tf_op | source)
XLA Modules:
  0.0 140.7 jit_solution(15998661899004031293)
XLA Ops:
  6.5 0.0 all-gather.2.cloned.1.call-start
  6.5 0.7 all-gather.2.cloned.1.call-update
  7.3 0.0 reduce-scatter.2.cloned.1.call-start
  7.3 0.7 convert_element_type.12
  8.0 0.2 copy.6
  8.2 8.0 %broadcast_multiply_fusion = bf16[1024,2,1024]{2,1,0:T(2,128)(2,1)} fusion(bf16[1024,2,1024]{2,1,0:T(2,128)(2,1)} %param.5, bf16[1024,2]{1,0:T(8,128)(2,1)S(1)} %copy.6), kind=kLoop, calls=%fused_computation.3 | loop fusion | flops 2097152 | bytes 8392704 | tf_op jit(solution)/shard_map/mul | solution.py:8
  16.2 0.0 copy-start
  16.2 0.0 copy-start.1
  16.2 77.1 %all-gather.2.cloned.1.call-done = bf16[2,1024,1024]{2,1,0:T(8,128)(2,1)} async-done(((bf16[2,16,1024]{2,1,0:T(8,128)(2,1)}), bf16[2,1024,1024]{2,1,0:T(8,128)(2,1)}) %all-gather.2.cloned.1.call-update) | async-done | bytes 4194320 | tf_op jit(solution)/shard_map/all_gather | solution.py:12
  93.3 9.3 %bitcast_convert_fusion = bf16[1024,1024]{1,0:T(8,128)(2,1)} fusion(bf16[2,1024,1024]{2,1,0:T(8,128)(2,1)} %all-gather.2.cloned.1.call-done, bf16[1024,2,1024]{2,1,0:T(2,128)(2,1)} %broadcast_multiply_fusion), kind=kOutput, calls=%fused_computation | convolution fusion | flops 4296015872 | bytes 10485760 | tf_op jit(solution)/shard_map/ptk,tkn->pn/dot_general | solution.py:9
  102.6 0.0 reduce-scatter.2.cloned.1.call-update
  102.7 29.1 %reduce-scatter.2.cloned.1.call-done = bf16[256,1024]{1,0:T(8,128)(2,1)} async-done(((bf16[1024,1024]{1,0:T(8,128)(2,1)}), bf16[256,1024]{1,0:T(8,128)(2,1)}) %reduce-scatter.2.cloned.1.call-update) | async-done | bytes 524304 | tf_op jit(solution)/shard_map/reduce_scatter | solution.py:15
  131.8 0.0 copy-done
  131.8 0.0 copy-done.1
  131.8 2.1 %divide_convert_fusion = bf16[256,1024]{1,0:T(8,128)(2,1)} fusion(bf16[256,1024]{1,0:T(8,128)(2,1)} %reduce-scatter.2.cloned.1.call-done, f32[256]{0:T(256)S(1)} %copy-done.1, f32[1024]{0:T(1024)S(1)} %copy-done), kind=kLoop, calls=%fused_computation.4 | loop fusion | flops 1048576 | bytes 1053696 | tf_op jit(solution)/shard_map/convert_element_type | solution.py:19
Async XLA Ops:
  6.5 86.8 %all-gather.2.cloned.1.call-start = ((), (), s32[]{:S(2)}) async-start(), calls=%async_computation.1 | async-start | bytes 4259840 | tf_op jit(solution)/shard_map/all_gather | solution.py:12
  7.3 124.5 %reduce-scatter.2.cloned.1.call-start = ((), (), s32[]{:S(2)}) async-start(), calls=%async_computation.2 | async-start | bytes 2621440 | tf_op jit(solution)/shard_map/reduce_scatter | solution.py:15
  16.2 115.6 %copy-start = (f32[1024]{0:T(1024)S(1)}, f32[1024]{0:T(1024)}, u32[]{:S(2)}) copy-start(f32[1024]{0:T(1024)} %param.9) | copy-start | bytes 12292
  16.2 115.6 %copy-start.1 = (f32[256]{0:T(256)S(1)}, f32[256]{0:T(256)}, u32[]{:S(2)}) copy-start(f32[256]{0:T(256)} %param.8) | copy-start | bytes 3076
Sparse Core Ops, SparseCore 0:
  10.1 83.1 all-gather.1
  102.8 28.9 reduce-scatter.1
where the time goes:
time: 141 us
  waiting for transfers between devices  107 us (76%)
  between operations  13.4 us (10%)
  other arithmetic  10.8 us (8%)
  matrix products  9.32 us (7%)
    all_gather x1, waiting for transfers between devices, on_device(): lax.all_gather(integrals, 'pair', axis=1, tiled=True)  77.1 us
    reduce_scatter x1, waiting for transfers between devices, on_device(): lax.psum_scatter(partial_value.astype(jnp.bfloat16), 'virt', scatter_dime...  29.1 us
    dot_general x1, matrix products, on_device(): jnp.einsum('ptk,tkn->pn', masked, lax.all_gather(integrals, 'pair', axis=...  9.32 us
    mul x1, other arithmetic, on_device(): masked = amplitudes * tile_mask.astype(jnp.bfloat16)[:, :, None]  8.03 us
  transfers between devices with their start and end apart: 2, of which 2 were waited for; matrix products, arithmetic and copies ran while one was open for 6% of the time, Pallas kernels for 0%

commit v1 on v0

v1 whole, which is shorter than its diff:
```python
import functools

import jax
import jax.numpy as jnp
from jax import lax
from jax.experimental import pallas as pl
from jax.experimental.pallas import tpu as pltpu
from jax.sharding import PartitionSpec as P

MESH = pl.DeviceIdType.MESH
XN, ZN, KN, YN = 4, 8, 2, 4
W = 128
F32, BF16 = jnp.float32, jnp.bfloat16
ZGROUPS = ((0, 1), (1, 2), (2, 4), (4, 8))


def kernel(amp, mask, vin, pe, ve, out, xbuf, lhs, vb, perm, mb, pb, snd2, s_p, s_m,
           r2a, r2b, r_p, r_m, h_p, h_m, own, asem, vsem, zs, zr, xs, xr, cs, cr, ys, yr):
    pairs = lhs.shape[0]
    rows = pairs // YN
    half = rows // 2
    depth = vin.shape[1]
    chunks = vin.shape[2] // W
    kdim = XN * ZN * KN * depth

    me = lax.axis_index("pair")
    j = lax.axis_index("virt")
    k = me % KN
    z = (me // KN) % ZN
    x = me // (KN * ZN)

    def dev(xx, zz, kk):
        return {"pair": (xx * ZN + zz) * KN + kk, "virt": j}

    def ydev(jj):
        return {"pair": me, "virt": jj}

    xp, xm, xo = (x + 1) % XN, (x + XN - 1) % XN, (x + 2) % XN
    jp, jm, jo = (j + 1) % YN, (j + YN - 1) % YN, (j + 2) % YN
    partner = dev(x, z, 1 - k)
    zpeer = [dev(x, (z + d) % ZN, k) for d in range(ZN)]

    def remote(src, dst, ss, rs, to):
        return pltpu.make_async_remote_copy(
            src_ref=src, dst_ref=dst, send_sem=ss, recv_sem=rs, device_id=to, device_id_type=MESH)

    parts = asem.shape[0]
    part_rows = amp.shape[0] // parts

    def amp_copy(q):
        sl = pl.ds(q * part_rows, part_rows)
        return pltpu.make_async_copy(amp.at[sl], xbuf.at[sl], asem.at[q])

    for q in range(parts):
        amp_copy(q).start()
    own_copy = pltpu.make_async_copy(vin, vb.at[:, x, z, k], vsem)
    own_copy.start()

    barrier = pltpu.get_barrier_semaphore()
    friends = zpeer[1:] + [dev(xp, z, k), dev(xm, z, k), partner, ydev(jp), ydev(jm)]
    for to in friends:
        pl.semaphore_signal(barrier, inc=1, device_id=to, device_id_type=MESH)

    r = lax.broadcasted_iota(jnp.int32, (256, 256), 0)
    s = lax.broadcasted_iota(jnp.int32, (256, 256), 1)
    target = (r & 15) * 16 + ((r >> 4) & 7) * 2 + (r >> 7)
    perm[...] = jnp.where(s == target, 1.0, 0.0).astype(BF16)
    for t in range(2):
        row = mask[t:t + 1, :].astype(F32)
        mb[t] = jnp.broadcast_to(row, (128, pairs)).T
    pb[...] = jnp.broadcast_to(pe[...], (128, rows)).T

    pl.semaphore_wait(barrier, len(friends))

    def zcopy(g, d):
        lo, hi = ZGROUPS[g]
        cols = pl.ds(lo * W, (hi - lo) * W)
        return remote(vin.at[:, :, cols], vb.at[:, x, z, k, :, cols], zs.at[g, d], zr.at[g, d], zpeer[d])

    for g in range(len(ZGROUPS)):
        for d in (4, 3, 5, 2, 6, 1, 7):
            zcopy(g, d).start()

    def zwait(g):
        for d in range(1, ZN):
            zcopy(g, d).wait_recv()

    def column(xx, cols):
        return vb.at[:, xx, :, k, :, cols]

    def csl(c):
        return pl.ds(pl.multiple_of(c * W, W), W)

    def xcopy(c, way):
        cols = csl(c)
        if way == 0:
            return remote(column(x, cols), column(x, cols), xs.at[c, 0], xr.at[c, 0], dev(xp, z, k))
        if way == 1:
            return remote(column(x, cols), column(x, cols), xs.at[c, 1], xr.at[c, 1], dev(xm, z, k))
        if way == 2:
            ref = vb.at[0, xm, :, k, :, cols]
            return remote(ref, ref, xs.at[c, 2], xr.at[c, 2], dev(xp, z, k))
        ref = vb.at[1, xp, :, k, :, cols]
        return remote(ref, ref, xs.at[c, 3], xr.at[c, 3], dev(xm, z, k))

    def ccopy(c, n):
        ref = column((x, xm, xp, xo)[n], csl(c))
        return remote(ref, ref, cs.at[c, n], cr.at[c, n], partner)

    def g2(c):
        xcopy(c, 0).start()
        xcopy(c, 1).start()
        ccopy(c, 0).start()

    def g3(c):
        xcopy(c, 0).wait_recv()
        xcopy(c, 2).start()
        ccopy(c, 1).start()
        xcopy(c, 1).wait_recv()
        xcopy(c, 3).start()
        ccopy(c, 2).start()

    def g4(c):
        xcopy(c, 2).wait_recv()
        xcopy(c, 3).wait_recv()
        ccopy(c, 3).start()

    def gdone(c):
        for n in range(4):
            ccopy(c, n).wait_recv()

    def relayout(q):
        amp_copy(q).wait()
        steps = part_rows // 512

        @pl.loop(0, steps)
        def _(i):
            base = pl.multiple_of(q * part_rows + i * 512, 512)
            ab = jnp.concatenate([xbuf[pl.ds(base, 256), :], xbuf[pl.ds(base + 256, 256), :]], axis=1)
            res = jnp.dot(perm[...], ab, preferred_element_type=F32)
            for b in range(2):
                p0 = pl.multiple_of((q * part_rows) // 16 + i * 32 + b * 16, 16)
                for t in range(2):
                    m = mb[t, pl.ds(p0, 16), :]
                    for kt in range(8):
                        o = t * 128 + kt * 16
                        lhs[pl.ds(p0, 16), pl.ds(t * kdim + kt * 128, 128)] = (
                            res[o:o + 16, b * 128:b * 128 + 128] * m).astype(BF16)

    def ycopy(c, n):
        a, b = pl.ds(0, half), pl.ds(half, half)
        src, dst, to = (
            (snd2.at[c, a], r2a.at[c], jm),
            (snd2.at[c, b], r2b.at[c], jp),
            (s_p.at[c, a], r_m.at[c, a], jp),
            (s_m.at[c, b], r_p.at[c, b], jm),
            (s_p.at[c, b], r_m.at[c, b], jp),
            (s_m.at[c, a], r_p.at[c, a], jm),
        )[n]
        return remote(src, dst, ys.at[c, n], yr.at[c, n], ydev(to))

    def compute(c):
        cols = csl(c)
        rhs0 = vb[0, :, :, :, :, cols].reshape(kdim, W)
        rhs1 = vb[1, :, :, :, :, cols].reshape(kdim, W)

        def part(d):
            sl = pl.ds(pl.multiple_of(d * rows, rows), rows)
            return (jnp.dot(lhs[sl, 0:kdim], rhs0, preferred_element_type=F32)
                    + jnp.dot(lhs[sl, kdim:2 * kdim], rhs1, preferred_element_type=F32))

        snd2[c] = part(jo).astype(BF16)
        ycopy(c, 0).start()
        ycopy(c, 1).start()
        res = part(jp)
        s_p[c, 0:half] = res[0:half].astype(BF16)
        h_p[c % 2] = res[half:]
        ycopy(c, 2).start()
        res = part(jm)
        s_m[c, half:rows] = res[half:].astype(BF16)
        h_m[c % 2] = res[0:half]
        ycopy(c, 3).start()
        own[c % 3] = part(j)

    def combine(c):
        ycopy(c, 1).wait_recv()
        s_p[c, half:rows] = (h_p[c % 2] + r2b[c].astype(F32)).astype(BF16)
        ycopy(c, 4).start()
        ycopy(c, 0).wait_recv()
        s_m[c, 0:half] = (h_m[c % 2] + r2a[c].astype(F32)).astype(BF16)
        ycopy(c, 5).start()

    def final(c):
        for n in (2, 3, 4, 5):
            ycopy(c, n).wait_recv()
        cols = csl(c)
        total = own[c % 3] + r_p[c].astype(F32) + r_m[c].astype(F32)
        out[:, cols] = (total / (ve[:, cols] - pb[...])).astype(BF16)

    relayout(0)
    own_copy.wait()
    zwait(0)
    g2(0)
    relayout(1)
    zwait(1)
    g2(1)
    g3(0)
    relayout(2)
    zwait(2)
    g2(2)
    g4(0)
    g3(1)
    g2(3)
    relayout(3)

    @pl.loop(0, chunks)
    def _(c):
        gdone(c)

        compute(c)

        @pl.when(c + 1 < chunks)
        def _():
            g4(c + 1)

        @pl.when(c + 2 < chunks)
        def _():
            g3(c + 2)

        @pl.when(c == 0)
        def _():
            zwait(3)

        @pl.when(c + 4 < chunks)
        def _():
            g2(c + 4)

        @pl.when(c > 0)
        def _():
            combine(c - 1)

        @pl.when(c > 1)
        def _():
            final(c - 2)

    combine(chunks - 1)
    final(chunks - 2)
    final(chunks - 1)

    for g in range(len(ZGROUPS)):
        for d in range(1, ZN):
            zcopy(g, d).wait_send()

    @pl.loop(0, chunks)
    def _(c):
        for n in range(4):
            xcopy(c, n).wait_send()
            ccopy(c, n).wait_send()
        for n in range(6):
            ycopy(c, n).wait_send()


def on_device(amplitudes, tile_mask, integrals, pair_energy, virt_energy):
    pairs, tiles, kdim = amplitudes.shape
    depth, ab = integrals.shape[1:]
    rows = pairs // YN
    half = rows // 2
    chunks = ab // W
    kt = kdim // 128
    amp = amplitudes.reshape(pairs, tiles, kt, 128).transpose(0, 2, 1, 3).reshape(pairs * kt * tiles, 128)
    vmem = pl.BlockSpec(memory_space=pltpu.VMEM)
    dma = pltpu.SemaphoreType.DMA
    return pl.pallas_call(
        kernel,
        out_shape=jax.ShapeDtypeStruct((rows, ab), BF16),
        in_specs=[pl.BlockSpec(memory_space=pl.ANY), vmem, vmem, vmem, vmem],
        out_specs=vmem,
        scratch_shapes=[
            pltpu.VMEM(amp.shape, BF16),
            pltpu.VMEM((pairs, tiles * kdim), BF16),
            pltpu.VMEM((tiles, XN, ZN, KN, depth, ab), BF16),
            pltpu.VMEM((256, 256), BF16),
            pltpu.VMEM((tiles, pairs, 128), F32),
            pltpu.VMEM((rows, 128), F32),
            pltpu.VMEM((chunks, rows, W), BF16),
            pltpu.VMEM((chunks, rows, W), BF16),
            pltpu.VMEM((chunks, rows, W), BF16),
            pltpu.VMEM((chunks, half, W), BF16),
            pltpu.VMEM((chunks, half, W), BF16),
            pltpu.VMEM((chunks, rows, W), BF16),
            pltpu.VMEM((chunks, rows, W), BF16),
            pltpu.VMEM((2, half, W), F32),
            pltpu.VMEM((2, half, W), F32),
            pltpu.VMEM((3, rows, W), F32),
            dma((4,)),
            dma,
            dma((len(ZGROUPS), ZN)),
            dma((len(ZGROUPS), ZN)),
            dma((chunks, 4)),
            dma((chunks, 4)),
            dma((chunks, 4)),
            dma((chunks, 4)),
            dma((chunks, 6)),
            dma((chunks, 6)),
        ],
        compiler_params=pltpu.CompilerParams(collective_id=0, has_side_effects=True),
        name="ladder",
    )(amp, tile_mask.T, integrals, pair_energy[None, :], virt_energy[None, :])


def solution(mesh):
    placed = (
        P("pair", "virt", None),
        P("pair", "virt"),
        P("virt", "pair", None),
        P(("pair", "virt")),
        P(),
    )
    return jax.shard_map(
        on_device, mesh=mesh, in_specs=placed, out_specs=P(("pair", "virt"), None), check_vma=False
    )
```

time: 141 us -> 61.7 us (0.44)
  waiting for transfers between devices: 107 us -> 0 us
  Pallas kernels: 0 us -> 59.6 us
  between operations: 13.4 us -> 0.01 us
  other arithmetic: 10.8 us -> 0 us
  matrix products: 9.32 us -> 0 us
  local copies, waits for them, and re-layouts: 0.21 us -> 1.87 us
    all_gather x1 -> x0, waiting for transfers between devices: 77.1 us -> none  [on_device(): lax.all_gather(integrals, 'pair', axis=1, tiled=True)]
    pallas_call x0 -> x1, Pallas kernels: none -> 59.6 us  [on_device(): pl.pallas_call(kernel, out_shape=jax.ShapeDtypeStruct((rows, ab), BF16),...]
    reduce_scatter x1 -> x0, waiting for transfers between devices: 29.1 us -> none  [on_device(): lax.psum_scatter(partial_value.astype(jnp.bfloat16), 'virt', scatter_dime...]
    dot_general x1 -> x0, matrix products: 9.32 us -> none  [on_device(): jnp.einsum('ptk,tkn->pn', masked, lax.all_gather(integrals, 'pair', axis=...]
    mul x1 -> x0, other arithmetic: 8.03 us -> none  [on_device(): masked = amplitudes * tile_mask.astype(jnp.bfloat16)[:, :, None]]
    convert_element_type x2 -> x0, other arithmetic: 2.81 us -> none  [the longest x1 2.1 us: on_device(): return (ladder / denom).astype(jnp.bfloat16)]
    unnamed x4 -> x1, local copies, waits for them, and re-layouts: 0.01 us -> 1.87 us
  transfers between devices with their start and end apart: 2 -> 0, of which waited for: 2 -> 0; matrix products, arithmetic and copies ran while one was open for 6% -> 0% of each run, Pallas kernels for 0% -> 0%
where the time goes in v1:
time: 61.7 us; the launch traced here: 61.5 us
  Pallas kernels  59.6 us (97%)
  local copies, waits for them, and re-layouts  1.87 us (3%)
    pallas_call x1, Pallas kernels, on_device(): pl.pallas_call(kernel, out_shape=jax.ShapeDtypeStruct((rows, ab), BF16),...  59.6 us
    unnamed x1, local copies, waits for them, and re-layouts  1.87 us

profile of v1, /device:TPU:1, one launch (start us, length us, event | category | flops | bytes accessed | tf_op | source)
XLA Modules:
  0.0 61.5 jit_solution(1030385373723048315)
XLA Ops:
  0.0 59.6 %ladder.1 = bf16[256,1024]{1,0:T(8,128)(2,1)} custom-call(bf16[16384,128]{1,0:T(8,128)(2,1)} %bitcast.8, s32[2,1024]{1,0:T(2,128)} %bitcast.9, bf16[2,16,1024]{2,1,0:T(8,128)(2,1)} %vin.1, f32[1,256]{1,0:T(1,128)} %bitcast.11, f32[1,1024]{1,0:T(1,128)} %bitcast.10), custom_call_target="tpu_custom_call" | custom-call | tf_op jit(solution)/shard_map/ladder/pallas_call | solution.py:273
  59.7 1.9 %copy.8 = bf16[256,1024]{1,0:T(8,128)(2,1)} copy(bf16[256,1024]{1,0:T(8,128)(2,1)} %ladder.1) | data formatting | bytes 1048576

commit v2 on v1

v2 whole, which is shorter than its diff:
```python
import functools

import jax
import jax.numpy as jnp
from jax import lax
from jax.experimental import pallas as pl
from jax.experimental.pallas import tpu as pltpu
from jax.sharding import PartitionSpec as P

MESH = pl.DeviceIdType.MESH
XN, ZN, KN, YN = 4, 8, 2, 4
W = 128
F32, BF16 = jnp.float32, jnp.bfloat16
GROUPS = ((0, 1, True), (1, 1, True), (2, 2, False), (4, 2, False), (6, 2, False))
NG = len(GROUPS)
PLAN = (
    ((0, 2),),
    ((2, 3), (3, 1), (4, 0), (1, 2)),
    ((2, 4), (3, 2), (4, 1), (2, 5), (2, 6)),
    ((3, 3), (4, 2)),
    ((3, 4), (4, 3), (3, 5), (3, 6)),
    ((4, 4),),
    ((4, 5), (4, 6)),
    (),
)
LAG, LAG2 = 2, 4


def kernel(amp, mask, vin, pe, ve, out, xbuf, lhs, vt, vb, perm, mb, pb, snd2, s_p, s_m,
           r2a, r2b, r_p, r_m, h_p, h_m, own, asem, tsem, vsem,
           es, er, qs, qr, ps, pr, ys, yr):
    pairs = lhs.shape[0]
    rows = pairs // YN
    half = rows // 2
    chunks, _, depth, _ = vt.shape
    kdim = XN * ZN * KN * depth

    me = lax.axis_index("pair")
    j = lax.axis_index("virt")
    k = me % KN
    z = (me // KN) % ZN
    x = me // (KN * ZN)

    def dev(dx, dz, kk):
        return {"pair": (((x + dx) % XN) * ZN + (z + dz) % ZN) * KN + kk, "virt": j}

    def ydev(jj):
        return {"pair": me, "virt": jj}

    def xa(d):
        return (x + d + XN) % XN

    def za(d):
        return (z + d + ZN) % ZN

    jp, jm, jo = (j + 1) % YN, (j + YN - 1) % YN, (j + 2) % YN
    partner = dev(0, 0, 1 - k)

    def remote(src, dst, ss, rs, to):
        return pltpu.make_async_remote_copy(
            src_ref=src, dst_ref=dst, send_sem=ss, recv_sem=rs, device_id=to, device_id_type=MESH)

    def same(ref, ss, rs, to):
        return remote(ref, ref, ss, rs, to)

    parts = asem.shape[0]
    part_rows = amp.shape[0] // parts

    def amp_copy(q):
        sl = pl.ds(q * part_rows, part_rows)
        return pltpu.make_async_copy(amp.at[sl], xbuf.at[sl], asem.at[q])

    def tile_copy(c):
        return pltpu.make_async_copy(vin.at[:, :, c * W:(c + 1) * W], vt.at[c], tsem.at[c])

    for c in range(chunks):
        tile_copy(c).start()
    for q in range(parts):
        amp_copy(q).start()

    barrier = pltpu.get_barrier_semaphore()
    friends = [dev(d, 0, kk) for d in range(1, XN) for kk in range(KN)]
    friends += [dev(0, d, kk) for d in range(1, ZN) for kk in range(KN)]
    friends += [partner, ydev(jp), ydev(jm)]
    for to in friends:
        pl.semaphore_signal(barrier, inc=1, device_id=to, device_id_type=MESH)

    for c in range(chunks):
        tile_copy(c).wait()
    own_copy = pltpu.make_async_copy(vt.at[:, k], vb.at[:, k, x, z, k], vsem)
    own_copy.start()

    r = lax.broadcasted_iota(jnp.int32, (256, 256), 0)
    s = lax.broadcasted_iota(jnp.int32, (256, 256), 1)
    target = (r & 15) * 16 + ((r >> 4) & 7) * 2 + (r >> 7)
    perm[...] = jnp.where(s == target, 1.0, 0.0).astype(BF16)
    for t in range(2):
        row = mask[t:t + 1, :].astype(F32)
        mb[t] = jnp.broadcast_to(row, (128, pairs)).T
    pb[...] = jnp.broadcast_to(pe[...], (128, rows)).T

    pl.semaphore_wait(barrier, len(friends))

    def gsl(g):
        return pl.ds(GROUPS[g][0], GROUPS[g][1])

    def first_x(g, d):
        return remote(vt.at[gsl(g), 0], vb.at[gsl(g), 0, x, z, k], es.at[g, d], er.at[g, d, k], dev(d, 0, 0))

    def first_z(g, d):
        return remote(vt.at[gsl(g), 1], vb.at[gsl(g), 1, x, z, k], es.at[g, 4 + d], er.at[g, d, k], dev(0, d, 1))

    def first_zd(g):
        return (4, 3, 5, 2, 6, 1, 7) if GROUPS[g][2] else (1, 7)

    def first_partner(g):
        return remote(vt.at[gsl(g), 1 - k], vb.at[gsl(g), 1 - k, x, z, k], es.at[g, 0], er.at[g, 0, k], partner)

    for g in range(NG):
        for d in first_zd(g):
            first_z(g, d).start()
        for d in (2, 1, 3):
            first_x(g, d).start()
        first_partner(g).start()

    def first_wait(g, ds):
        for d in ds:
            for kk in range(KN):
                remote(vt.at[gsl(g), 0], vb.at[gsl(g), 0, x, z, kk], es.at[g, d], er.at[g, d, kk], partner).wait_recv()
        remote(vt.at[gsl(g), 0], vb.at[gsl(g), 0, x, z, 0], es.at[g, 0], er.at[g, 0, 1 - k], partner).wait_recv()

    def row(g, dz, xs=slice(None)):
        return vb.at[gsl(g), 0, xs, za(dz)]

    def row_direct(g, d):
        return same(row(g, 0), qs.at[g, d], qr.at[g, d], dev(0, d, 0))

    def row_step(g, n, way):
        far = n == 3
        if way == 0:
            ref = row(g, -n, slice(0, XN // 2) if far else slice(None))
            return same(ref, qs.at[g, 2 * n], qr.at[g, 2 * n], dev(0, 1, 0))
        ref = row(g, n, slice(XN // 2, XN) if far else slice(None))
        return same(ref, qs.at[g, 2 * n + 1], qr.at[g, 2 * n + 1], dev(0, ZN - 1, 0))

    def row_partner(g, dz):
        return same(row(g, dz), ps.at[g, dz % ZN], pr.at[g, dz % ZN], partner)

    def ring_step(g, n, way):
        if way == 0:
            ref = vb.at[gsl(g), 1, x, za(-n)]
            return same(ref, qs.at[g, 2 * n - 2], qr.at[g, 2 * n - 2], dev(0, 1, 1))
        ref = vb.at[gsl(g), 1, x, za(n)]
        return same(ref, qs.at[g, 2 * n - 1], qr.at[g, 2 * n - 1], dev(0, ZN - 1, 1))

    def col(g, dx, zs=slice(None)):
        return vb.at[gsl(g), 1, xa(dx), zs]

    def col_direct(g, d):
        return same(col(g, 0), qs.at[g, 5 + d], qr.at[g, 5 + d], dev(d, 0, 1))

    def col_forward(g, way):
        if way == 0:
            return same(col(g, -1, slice(0, ZN // 2)), qs.at[g, 9], qr.at[g, 9], dev(1, 0, 1))
        return same(col(g, 1, slice(ZN // 2, ZN)), qs.at[g, 10], qr.at[g, 10], dev(XN - 1, 0, 1))

    def col_partner(g, dx):
        return same(col(g, dx), ps.at[g, dx % XN], pr.at[g, dx % XN], partner)

    def rows_all(g):
        if GROUPS[g][2]:
            return [row_direct(g, d) for d in (4, 3, 5, 2, 6, 1, 7)]
        return [row_step(g, n, w) for n in range(4) for w in range(2)]

    def cols_all(g):
        if GROUPS[g][2]:
            return [col_direct(g, d) for d in (2, 1, 3)]
        out = [ring_step(g, n, w) for n in (1, 2) for w in range(2)] + [ring_step(g, 3, 0)]
        return out + [col_direct(g, 1), col_direct(g, 3), col_forward(g, 0), col_forward(g, 1)]

    def stage_rows(g, st):
        direct = GROUPS[g][2]
        if st == 0:
            first_wait(g, (1, 2, 3))
            for cp in rows_all(g) if direct else (row_step(g, 0, 0), row_step(g, 0, 1)):
                cp.start()
            row_partner(g, 0).start()
        elif direct and st == 1:
            for d in (1, 7, 2, 6, 3, 5, 4):
                row_direct(g, d).wait_recv()
                row_partner(g, -d).start()
        elif not direct and st <= 3:
            row_step(g, st - 1, 0).wait_recv()
            row_step(g, st, 0).start()
            row_partner(g, -st).start()
            row_step(g, st - 1, 1).wait_recv()
            row_step(g, st, 1).start()
            row_partner(g, st).start()
        elif not direct and st == 4:
            row_step(g, 3, 0).wait_recv()
            row_step(g, 3, 1).wait_recv()
            row_partner(g, 4).start()
        elif st == (2 if direct else 6):
            for d in range(XN):
                col_partner(g, d).wait_recv()

    def stage_cols(g, st):
        direct = GROUPS[g][2]
        if st == 0:
            first_wait(g, range(1, ZN) if direct else (1, 7))
        if not direct and st <= 2:
            if st:
                ring_step(g, st, 0).wait_recv()
            ring_step(g, st + 1, 0).start()
            if st:
                ring_step(g, st, 1).wait_recv()
            if st < 2:
                ring_step(g, st + 1, 1).start()
        elif st == (0 if direct else 3):
            if not direct:
                ring_step(g, 3, 0).wait_recv()
            for d in (2, 1, 3) if direct else (1, 3):
                col_direct(g, d).start()
            col_partner(g, 0).start()
        elif direct and st == 1:
            for d in (1, 3, 2):
                col_direct(g, d).wait_recv()
                col_partner(g, -d).start()
        elif not direct and st == 4:
            col_direct(g, 1).wait_recv()
            col_forward(g, 0).start()
            col_partner(g, -1).start()
            col_direct(g, 3).wait_recv()
            col_forward(g, 1).start()
            col_partner(g, 1).start()
        elif not direct and st == 5:
            col_forward(g, 0).wait_recv()
            col_forward(g, 1).wait_recv()
            col_partner(g, 2).start()
        elif st == (2 if direct else 6):
            for d in range(ZN):
                row_partner(g, d).wait_recv()

    def stages(*steps):
        @pl.when(k == 0)
        def _():
            for g, st in steps:
                stage_rows(g, st)

        @pl.when(k == 1)
        def _():
            for g, st in steps:
                stage_cols(g, st)

    def relayout(q):
        amp_copy(q).wait()
        steps = part_rows // 512

        @pl.loop(0, steps)
        def _(i):
            base = pl.multiple_of(q * part_rows + i * 512, 512)
            ab = jnp.concatenate([xbuf[pl.ds(base, 256), :], xbuf[pl.ds(base + 256, 256), :]], axis=1)
            res = jnp.dot(perm[...], ab, preferred_element_type=F32)
            for b in range(2):
                p0 = pl.multiple_of((q * part_rows) // 16 + i * 32 + b * 16, 16)
                for t in range(2):
                    m = mb[t, pl.ds(p0, 16), :]
                    for kt in range(8):
                        o = t * 128 + kt * 16
                        lhs[pl.ds(p0, 16), pl.ds(t * kdim + kt * 128, 128)] = (
                            res[o:o + 16, b * 128:b * 128 + 128] * m).astype(BF16)

    def ycopy(c, n):
        a, b = pl.ds(0, half), pl.ds(half, half)
        src, dst, to = (
            (snd2.at[c, a], r2a.at[c], jm),
            (snd2.at[c, b], r2b.at[c], jp),
            (s_p.at[c, a], r_m.at[c, a], jp),
            (s_m.at[c, b], r_p.at[c, b], jm),
            (s_p.at[c, b], r_m.at[c, b], jp),
            (s_m.at[c, a], r_p.at[c, a], jm),
        )[n]
        return remote(src, dst, ys.at[c, n], yr.at[c, n], ydev(to))

    def compute(c):
        rhs0 = vb[c, 0].reshape(kdim, W)
        rhs1 = vb[c, 1].reshape(kdim, W)

        def part(d):
            sl = pl.ds(pl.multiple_of(d * rows, rows), rows)
            return (jnp.dot(lhs[sl, 0:kdim], rhs0, preferred_element_type=F32)
                    + jnp.dot(lhs[sl, kdim:2 * kdim], rhs1, preferred_element_type=F32))

        snd2[c] = part(jo).astype(BF16)
        ycopy(c, 0).start()
        ycopy(c, 1).start()
        res = part(jp)
        s_p[c, 0:half] = res[0:half].astype(BF16)
        h_p[c % (LAG + 1)] = res[half:]
        ycopy(c, 2).start()
        res = part(jm)
        s_m[c, half:rows] = res[half:].astype(BF16)
        h_m[c % (LAG + 1)] = res[0:half]
        ycopy(c, 3).start()
        own[c % (LAG2 + 1)] = part(j)

    def combine(c):
        ycopy(c, 1).wait_recv()
        s_p[c, half:rows] = (h_p[c % (LAG + 1)] + r2b[c].astype(F32)).astype(BF16)
        ycopy(c, 4).start()
        ycopy(c, 0).wait_recv()
        s_m[c, 0:half] = (h_m[c % (LAG + 1)] + r2a[c].astype(F32)).astype(BF16)
        ycopy(c, 5).start()

    def final(c):
        for n in (2, 3, 4, 5):
            ycopy(c, n).wait_recv()
        cols = pl.ds(pl.multiple_of(c * W, W), W)
        total = own[c % (LAG2 + 1)] + r_p[c].astype(F32) + r_m[c].astype(F32)
        out[:, cols] = (total / (ve[:, cols] - pb[...])).astype(BF16)

    relayout(0)
    own_copy.wait()
    relayout(1)
    stages((0, 0), (1, 0))
    relayout(2)
    stages((2, 0), (0, 1))
    relayout(3)
    stages((2, 1), (1, 1), (2, 2), (3, 0))

    @pl.loop(0, chunks)
    def _(c):
        for cc, steps in enumerate(PLAN):
            if steps:
                @pl.when(c == cc)
                def _():
                    stages(*steps)

        compute(c)

        @pl.when(c >= LAG)
        def _():
            combine(c - LAG)

        @pl.when(c >= LAG2)
        def _():
            final(c - LAG2)

    for n in range(LAG, 0, -1):
        combine(chunks - n)
    for n in range(LAG2, 0, -1):
        final(chunks - n)

    for g in range(NG):
        for d in first_zd(g):
            first_z(g, d).wait_send()
        for d in (1, 2, 3):
            first_x(g, d).wait_send()
        first_partner(g).wait_send()

    @pl.when(k == 0)
    def _():
        for g in range(NG):
            for cp in rows_all(g) + [row_partner(g, d) for d in range(ZN)]:
                cp.wait_send()

    @pl.when(k == 1)
    def _():
        for g in range(NG):
            for cp in cols_all(g) + [col_partner(g, d) for d in range(XN)]:
                cp.wait_send()

    @pl.loop(0, chunks)
    def _(c):
        for n in range(6):
            ycopy(c, n).wait_send()


def on_device(amplitudes, tile_mask, integrals, pair_energy, virt_energy):
    pairs, tiles, kdim = amplitudes.shape
    depth, ab = integrals.shape[1:]
    rows = pairs // YN
    half = rows // 2
    chunks = ab // W
    kt = kdim // 128
    amp = amplitudes.reshape(pairs, tiles, kt, 128).transpose(0, 2, 1, 3).reshape(pairs * kt * tiles, 128)
    vmem = pl.BlockSpec(memory_space=pltpu.VMEM)
    dma = pltpu.SemaphoreType.DMA
    return pl.pallas_call(
        kernel,
        out_shape=jax.ShapeDtypeStruct((rows, ab), BF16),
        in_specs=[pl.BlockSpec(memory_space=pl.ANY), vmem, pl.BlockSpec(memory_space=pl.ANY), vmem, vmem],
        out_specs=vmem,
        scratch_shapes=[
            pltpu.VMEM(amp.shape, BF16),
            pltpu.VMEM((pairs, tiles * kdim), BF16),
            pltpu.VMEM((chunks, tiles, depth, W), BF16),
            pltpu.VMEM((chunks, tiles, XN, ZN, KN, depth, W), BF16),
            pltpu.VMEM((256, 256), BF16),
            pltpu.VMEM((tiles, pairs, 128), F32),
            pltpu.VMEM((rows, 128), F32),
            pltpu.VMEM((chunks, rows, W), BF16),
            pltpu.VMEM((chunks, rows, W), BF16),
            pltpu.VMEM((chunks, rows, W), BF16),
            pltpu.VMEM((chunks, half, W), BF16),
            pltpu.VMEM((chunks, half, W), BF16),
            pltpu.VMEM((chunks, rows, W), BF16),
            pltpu.VMEM((chunks, rows, W), BF16),
            pltpu.VMEM((LAG + 1, half, W), F32),
            pltpu.VMEM((LAG + 1, half, W), F32),
            pltpu.VMEM((LAG2 + 1, rows, W), F32),
            dma((4,)),
            dma((chunks,)),
            dma,
            dma((NG, 12)),
            dma((NG, ZN, KN)),
            dma((NG, 11)),
            dma((NG, 11)),
            dma((NG, ZN)),
            dma((NG, ZN)),
            dma((chunks, 6)),
            dma((chunks, 6)),
        ],
        compiler_params=pltpu.CompilerParams(collective_id=0, has_side_effects=True),
        name="ladder",
    )(amp, tile_mask.T, integrals, pair_energy[None, :], virt_energy[None, :])


def solution(mesh):
    placed = (
        P("pair", "virt", None),
        P("pair", "virt"),
        P("virt", "pair", None),
        P(("pair", "virt")),
        P(),
    )
    return jax.shard_map(
        on_device, mesh=mesh, in_specs=placed, out_specs=P(("pair", "virt"), None), check_vma=False
    )
```

time: 61.7 us -> 64.6 us (1.047)
  Pallas kernels: 59.6 us -> 62.3 us
    pallas_call x1, Pallas kernels: 59.6 us -> 62.3 us  [on_device(): pl.pallas_call(kernel, out_shape=jax.ShapeDtypeStruct((rows, ab), BF16),...]
where the time goes in v2:
time: 64.6 us; the launch traced here: 64.2 us
  Pallas kernels  62.3 us (96%)
  local copies, waits for them, and re-layouts  1.87 us (3%)
    pallas_call x1, Pallas kernels, on_device(): pl.pallas_call(kernel, out_shape=jax.ShapeDtypeStruct((rows, ab), BF16),...  62.3 us
    unnamed x1, local copies, waits for them, and re-layouts  1.87 us

profile of v2, /device:TPU:1, one launch (start us, length us, event | category | flops | bytes accessed | tf_op | source)
XLA Modules:
  0.0 64.2 jit_solution(6695678327773673373)
XLA Ops:
  0.0 62.3 %ladder.1 = bf16[256,1024]{1,0:T(8,128)(2,1)} custom-call(bf16[16384,128]{1,0:T(8,128)(2,1)} %bitcast.8, s32[2,1024]{1,0:T(2,128)} %bitcast.9, bf16[2,16,1024]{2,1,0:T(8,128)(2,1)} %vin.1, f32[1,256]{1,0:T(1,128)} %bitcast.11, f32[1,1024]{1,0:T(1,128)} %bitcast.10), custom_call_target="tpu_custom_call" | custom-call | tf_op jit(solution)/shard_map/ladder/pallas_call | solution.py:389
  62.3 1.9 %copy.8 = bf16[256,1024]{1,0:T(8,128)(2,1)} copy(bf16[256,1024]{1,0:T(8,128)(2,1)} %ladder.1) | data formatting | bytes 1048576

commit v3 on v2

--- a/solution.py
+++ b/solution.py
@@ -11,24 +11,32 @@
 XN, ZN, KN, YN = 4, 8, 2, 4
 W = 128
 F32, BF16 = jnp.float32, jnp.bfloat16
-GROUPS = ((0, 1, True), (1, 1, True), (2, 2, False), (4, 2, False), (6, 2, False))
+NP = 3
+FIRST = ((0, 1), (1, 2))
+GROUPS = ((3, 2, False), (5, 3, False))
 NG = len(GROUPS)
+PRE = (
+    (),
+    (),
+    (),
+    (('Q', 0, 0), ('Q', 1, 0), ('P', 0, 0), ('P', 1, 0), ('P', 2, 0), ('Q', 0, 1), ('P', 0, 1), ('Q', 1, 1), ('P', 1, 1), ('P', 0, 2), ('Q', 0, 2), ('Q', 1, 2), ('P', 2, 1)),
+)
 PLAN = (
-    ((0, 2),),
-    ((2, 3), (3, 1), (4, 0), (1, 2)),
-    ((2, 4), (3, 2), (4, 1), (2, 5), (2, 6)),
-    ((3, 3), (4, 2)),
-    ((3, 4), (4, 3), (3, 5), (3, 6)),
-    ((4, 4),),
-    ((4, 5), (4, 6)),
-    (),
+    ((('P', 0, 3),), (('P', 1, 2),), (), (('Q', 0, 3),)),
+    ((('Q', 1, 3), ('P', 1, 3)), (('P', 2, 2),), (), ()),
+    ((('P', 2, 3),), (('Q', 0, 4), ('Q', 1, 4)), (), ()),
+    ((('Q', 0, 5), ('Q', 0, 6)), (), (), (('Q', 1, 5),)),
+    ((), (), (), ()),
+    ((('Q', 1, 6),), (), (), ()),
+    ((), (), (), ()),
+    ((), (), (), ()),
 )
 LAG, LAG2 = 2, 4
 
 
 def kernel(amp, mask, vin, pe, ve, out, xbuf, lhs, vt, vb, perm, mb, pb, snd2, s_p, s_m,
            r2a, r2b, r_p, r_m, h_p, h_m, own, asem, tsem, vsem,
-           es, er, qs, qr, ps, pr, ys, yr):
+           fs, fr, cs, cr, ks, kr, es, er, qs, qr, ps, pr, ys, yr):
     pairs = lhs.shape[0]
     rows = pairs // YN
     half = rows // 2
@@ -99,6 +107,25 @@
         mb[t] = jnp.broadcast_to(row, (128, pairs)).T
     pb[...] = jnp.broadcast_to(pe[...], (128, rows)).T
 
+    def relayout(q):
+        amp_copy(q).wait()
+        steps = part_rows // 512
+
+        @pl.loop(0, steps)
+        def _(i):
+            base = pl.multiple_of(q * part_rows + i * 512, 512)
+            ab = jnp.concatenate([xbuf[pl.ds(base, 256), :], xbuf[pl.ds(base + 256, 256), :]], axis=1)
+            res = jnp.dot(perm[...], ab, preferred_element_type=F32)
+            for b in range(2):
+                p0 = pl.multiple_of((q * part_rows) // 16 + i * 32 + b * 16, 16)
+                for t in range(2):
+                    m = mb[t, pl.ds(p0, 16), :]
+                    for kt in range(8):
+                        o = t * 128 + kt * 16
+                        lhs[pl.ds(p0, 16), pl.ds(t * kdim + kt * 128, 128)] = (
+                            res[o:o + 16, b * 128:b * 128 + 128] * m).astype(BF16)
+
+    relayout(0)
     pl.semaphore_wait(barrier, len(friends))
 
     def gsl(g):
@@ -116,12 +143,73 @@
     def first_partner(g):
         return remote(vt.at[gsl(g), 1 - k], vb.at[gsl(g), 1 - k, x, z, k], es.at[g, 0], er.at[g, 0, k], partner)
 
+    def fsl(f):
+        return pl.ds(FIRST[f][0], FIRST[f][1])
+
+    def p_first(f, d, t):
+        return remote(vt.at[fsl(f), t], vb.at[fsl(f), t, x, z, k], fs.at[f, d, t], fr.at[f, d, k], dev(0, d, t))
+
+    def p_partner_first(f):
+        return remote(vt.at[fsl(f), 1 - k], vb.at[fsl(f), 1 - k, x, z, k], fs.at[f, 0, 0], fr.at[f, 0, k], partner)
+
+    def p_first_wait(f):
+        def got(d, kk):
+            remote(vt.at[fsl(f), 0], vb.at[fsl(f), k, x, za(-d), kk], fs.at[f, d, 0], fr.at[f, d, kk], partner).wait_recv()
+
+        for d in range(1, ZN):
+            for kk in range(KN):
+                got(d, kk)
+        got(0, 1 - k)
+
+    def p_col(c, dx, zs=slice(None)):
+        return vb.at[c, k, xa(dx), zs]
+
+    def p_x(c, n):
+        if n < 2:
+            return same(p_col(c, 0), cs.at[c, n], cr.at[c, n], dev((1, XN - 1)[n], 0, k))
+        if n == 2:
+            return same(p_col(c, -1, slice(0, ZN // 2)), cs.at[c, 2], cr.at[c, 2], dev(1, 0, k))
+        return same(p_col(c, 1, slice(ZN // 2, ZN)), cs.at[c, 3], cr.at[c, 3], dev(XN - 1, 0, k))
+
+    def p_partner(c, dx):
+        return same(p_col(c, dx), ks.at[c, dx % XN], kr.at[c, dx % XN], partner)
+
+    def p_stage(c, st):
+        if st == 0:
+            for f, (c0, _) in enumerate(FIRST):
+                if c == c0:
+                    p_first_wait(f)
+            p_x(c, 0).start()
+            p_x(c, 1).start()
+            p_partner(c, 0).start()
+        elif st == 1:
+            for n, dx in ((0, -1), (1, 1)):
+                p_x(c, n).wait_recv()
+                p_x(c, n + 2).start()
+                p_partner(c, dx).start()
+        elif st == 2:
+            p_x(c, 2).wait_recv()
+            p_x(c, 3).wait_recv()
+            p_partner(c, 2).start()
+        else:
+            for d in range(XN):
+                p_partner(c, d).wait_recv()
+
+    def start_p(f):
+        for d in (4, 3, 5, 2, 6, 1, 7):
+            for t in range(2):
+                p_first(f, d, t).start()
+        p_partner_first(f).start()
+
+    start_p(0)
     for g in range(NG):
         for d in first_zd(g):
             first_z(g, d).start()
         for d in (2, 1, 3):
             first_x(g, d).start()
         first_partner(g).start()
+    for f in range(1, len(FIRST)):
+        start_p(f)
 
     def first_wait(g, ds):
         for d in ds:
@@ -241,34 +329,18 @@
             for d in range(ZN):
                 row_partner(g, d).wait_recv()
 
-    def stages(*steps):
-        @pl.when(k == 0)
-        def _():
-            for g, st in steps:
-                stage_rows(g, st)
-
-        @pl.when(k == 1)
-        def _():
-            for g, st in steps:
-                stage_cols(g, st)
-
-    def relayout(q):
-        amp_copy(q).wait()
-        steps = part_rows // 512
-
-        @pl.loop(0, steps)
-        def _(i):
-            base = pl.multiple_of(q * part_rows + i * 512, 512)
-            ab = jnp.concatenate([xbuf[pl.ds(base, 256), :], xbuf[pl.ds(base + 256, 256), :]], axis=1)
-            res = jnp.dot(perm[...], ab, preferred_element_type=F32)
-            for b in range(2):
-                p0 = pl.multiple_of((q * part_rows) // 16 + i * 32 + b * 16, 16)
-                for t in range(2):
-                    m = mb[t, pl.ds(p0, 16), :]
-                    for kt in range(8):
-                        o = t * 128 + kt * 16
-                        lhs[pl.ds(p0, 16), pl.ds(t * kdim + kt * 128, 128)] = (
-                            res[o:o + 16, b * 128:b * 128 + 128] * m).astype(BF16)
+    def stages(steps):
+        for kind, n, st in steps:
+            if kind == "P":
+                p_stage(n, st)
+            else:
+                @pl.when(k == 0)
+                def _():
+                    stage_rows(n, st)
+
+                @pl.when(k == 1)
+                def _():
+                    stage_cols(n, st)
 
     def ycopy(c, n):
         a, b = pl.ds(0, half), pl.ds(half, half)
@@ -282,26 +354,30 @@
         )[n]
         return remote(src, dst, ys.at[c, n], yr.at[c, n], ydev(to))
 
-    def compute(c):
-        rhs0 = vb[c, 0].reshape(kdim, W)
-        rhs1 = vb[c, 1].reshape(kdim, W)
+    def compute(c, slot):
 
         def part(d):
             sl = pl.ds(pl.multiple_of(d * rows, rows), rows)
+            rhs0 = vb[c, 0].reshape(kdim, W)
+            rhs1 = vb[c, 1].reshape(kdim, W)
             return (jnp.dot(lhs[sl, 0:kdim], rhs0, preferred_element_type=F32)
                     + jnp.dot(lhs[sl, kdim:2 * kdim], rhs1, preferred_element_type=F32))
 
+        slot(0)
         snd2[c] = part(jo).astype(BF16)
         ycopy(c, 0).start()
         ycopy(c, 1).start()
+        slot(1)
         res = part(jp)
         s_p[c, 0:half] = res[0:half].astype(BF16)
         h_p[c % (LAG + 1)] = res[half:]
         ycopy(c, 2).start()
+        slot(2)
         res = part(jm)
         s_m[c, half:rows] = res[half:].astype(BF16)
         h_m[c % (LAG + 1)] = res[0:half]
         ycopy(c, 3).start()
+        slot(3)
         own[c % (LAG2 + 1)] = part(j)
 
     def combine(c):
@@ -319,24 +395,22 @@
         total = own[c % (LAG2 + 1)] + r_p[c].astype(F32) + r_m[c].astype(F32)
         out[:, cols] = (total / (ve[:, cols] - pb[...])).astype(BF16)
 
-    relayout(0)
     own_copy.wait()
-    relayout(1)
-    stages((0, 0), (1, 0))
-    relayout(2)
-    stages((2, 0), (0, 1))
-    relayout(3)
-    stages((2, 1), (1, 1), (2, 2), (3, 0))
+    stages(PRE[0])
+    for q in range(1, parts):
+        relayout(q)
+        stages(PRE[q])
 
     @pl.loop(0, chunks)
     def _(c):
-        for cc, steps in enumerate(PLAN):
-            if steps:
-                @pl.when(c == cc)
-                def _():
-                    stages(*steps)
-
-        compute(c)
+        def slot(n):
+            for cc, slots in enumerate(PLAN):
+                if slots[n]:
+                    @pl.when(c == cc)
+                    def _():
+                        stages(slots[n])
+
+        compute(c, slot)
 
         @pl.when(c >= LAG)
         def _():
@@ -357,6 +431,17 @@
         for d in (1, 2, 3):
             first_x(g, d).wait_send()
         first_partner(g).wait_send()
+    for f in range(len(FIRST)):
+        for d in range(1, ZN):
+            for t in range(2):
+                p_first(f, d, t).wait_send()
+        p_partner_first(f).wait_send()
+
+    @pl.loop(0, NP)
+    def _(c):
+        for n in range(4):
+            p_x(c, n).wait_send()
+            p_partner(c, n).wait_send()
 
     @pl.when(k == 0)
     def _():
@@ -412,6 +497,12 @@
             dma((4,)),
             dma((chunks,)),
             dma,
+            dma((len(FIRST), ZN, KN)),
+            dma((len(FIRST), ZN, KN)),
+            dma((NP, 4)),
+            dma((NP, 4)),
+            dma((NP, 4)),
+            dma((NP, 4)),
             dma((NG, 12)),
             dma((NG, ZN, KN)),
             dma((NG, 11)),

time: 64.6 us -> 56.6 us (0.88)
  Pallas kernels: 62.3 us -> 54.5 us
    pallas_call x1, Pallas kernels: 62.3 us -> 54.5 us  [on_device(): pl.pallas_call(kernel, out_shape=jax.ShapeDtypeStruct((rows, ab), BF16),...]
where the time goes in v3:
time: 56.6 us; the launch traced here: 56.4 us
  Pallas kernels  54.5 us (96%)
  local copies, waits for them, and re-layouts  1.87 us (3%)
    pallas_call x1, Pallas kernels, on_device(): pl.pallas_call(kernel, out_shape=jax.ShapeDtypeStruct((rows, ab), BF16),...  54.5 us
    unnamed x1, local copies, waits for them, and re-layouts  1.87 us

profile of v3, /device:TPU:1, one launch (start us, length us, event | category | flops | bytes accessed | tf_op | source)
XLA Modules:
  0.0 56.4 jit_solution(15259924545751147694)
XLA Ops:
  0.0 54.5 %ladder.1 = bf16[256,1024]{1,0:T(8,128)(2,1)} custom-call(bf16[16384,128]{1,0:T(8,128)(2,1)} %bitcast.8, s32[2,1024]{1,0:T(2,128)} %bitcast.9, bf16[2,16,1024]{2,1,0:T(8,128)(2,1)} %vin.1, f32[1,256]{1,0:T(1,128)} %bitcast.11, f32[1,1024]{1,0:T(1,128)} %bitcast.10), custom_call_target="tpu_custom_call" | custom-call | tf_op jit(solution)/shard_map/ladder/pallas_call | solution.py:474
  54.5 1.9 %copy.8 = bf16[256,1024]{1,0:T(8,128)(2,1)} copy(bf16[256,1024]{1,0:T(8,128)(2,1)} %ladder.1) | data formatting | bytes 1048576

commit v4 on v3

--- a/solution.py
+++ b/solution.py
@@ -21,21 +21,21 @@
     (),
     (('Q', 0, 0), ('Q', 1, 0), ('P', 0, 0), ('P', 1, 0), ('P', 2, 0), ('Q', 0, 1), ('P', 0, 1), ('Q', 1, 1), ('P', 1, 1), ('P', 0, 2), ('Q', 0, 2), ('Q', 1, 2), ('P', 2, 1)),
 )
+BLOCKS = ((0, 1), (1, 1), (2, 1), (3, 2), (5, 2), (7, 1))
 PLAN = (
     ((('P', 0, 3),), (('P', 1, 2),), (), (('Q', 0, 3),)),
     ((('Q', 1, 3), ('P', 1, 3)), (('P', 2, 2),), (), ()),
     ((('P', 2, 3),), (('Q', 0, 4), ('Q', 1, 4)), (), ()),
     ((('Q', 0, 5), ('Q', 0, 6)), (), (), (('Q', 1, 5),)),
-    ((), (), (), ()),
     ((('Q', 1, 6),), (), (), ()),
     ((), (), (), ()),
-    ((), (), (), ()),
 )
-LAG, LAG2 = 2, 4
-
-
-def kernel(amp, mask, vin, pe, ve, out, xbuf, lhs, vt, vb, perm, mb, pb, snd2, s_p, s_m,
-           r2a, r2b, r_p, r_m, h_p, h_m, own, asem, tsem, vsem,
+NB = len(BLOCKS)
+LAG, LAG2 = 1, 3
+
+
+def kernel(amp, mask_in, vin, pe_in, ve_in, out, mask, pe, ve, xbuf, lhs, vt, vb, perm, mb, pb, snd2, s_p, s_m,
+           r2a, r2b, r_p, r_m, h_p, h_m, own, asem, tsem, isem, vsem,
            fs, fr, cs, cr, ks, kr, es, er, qs, qr, ps, pr, ys, yr):
     pairs = lhs.shape[0]
     rows = pairs // YN
@@ -81,11 +81,6 @@
     def tile_copy(c):
         return pltpu.make_async_copy(vin.at[:, :, c * W:(c + 1) * W], vt.at[c], tsem.at[c])
 
-    for c in range(chunks):
-        tile_copy(c).start()
-    for q in range(parts):
-        amp_copy(q).start()
-
     barrier = pltpu.get_barrier_semaphore()
     friends = [dev(d, 0, kk) for d in range(1, XN) for kk in range(KN)]
     friends += [dev(0, d, kk) for d in range(1, ZN) for kk in range(KN)]
@@ -94,6 +89,14 @@
         pl.semaphore_signal(barrier, inc=1, device_id=to, device_id_type=MESH)
 
     for c in range(chunks):
+        tile_copy(c).start()
+    for q in range(parts):
+        amp_copy(q).start()
+    small = [pltpu.make_async_copy(src, dst, isem.at[i])
+             for i, (src, dst) in enumerate(((mask_in, mask), (pe_in, pe), (ve_in, ve)))]
+    for cp in small:
+        cp.start()
+    for c in range(chunks):
         tile_copy(c).wait()
     own_copy = pltpu.make_async_copy(vt.at[:, k], vb.at[:, k, x, z, k], vsem)
     own_copy.start()
@@ -102,6 +105,8 @@
     s = lax.broadcasted_iota(jnp.int32, (256, 256), 1)
     target = (r & 15) * 16 + ((r >> 4) & 7) * 2 + (r >> 7)
     perm[...] = jnp.where(s == target, 1.0, 0.0).astype(BF16)
+    for cp in small:
+        cp.wait()
     for t in range(2):
         row = mask[t:t + 1, :].astype(F32)
         mb[t] = jnp.broadcast_to(row, (128, pairs)).T
@@ -111,7 +116,7 @@
         amp_copy(q).wait()
         steps = part_rows // 512
 
-        @pl.loop(0, steps)
+        @pl.loop(0, steps, unroll=2)
         def _(i):
             base = pl.multiple_of(q * part_rows + i * 512, 512)
             ab = jnp.concatenate([xbuf[pl.ds(base, 256), :], xbuf[pl.ds(base + 256, 256), :]], axis=1)
@@ -342,58 +347,72 @@
                 def _():
                     stage_cols(n, st)
 
-    def ycopy(c, n):
-        a, b = pl.ds(0, half), pl.ds(half, half)
+    def ycopy(b, n):
+        c = pl.ds(*BLOCKS[b])
+        lo, hi = pl.ds(0, half), pl.ds(half, half)
         src, dst, to = (
-            (snd2.at[c, a], r2a.at[c], jm),
-            (snd2.at[c, b], r2b.at[c], jp),
-            (s_p.at[c, a], r_m.at[c, a], jp),
-            (s_m.at[c, b], r_p.at[c, b], jm),
-            (s_p.at[c, b], r_m.at[c, b], jp),
-            (s_m.at[c, a], r_p.at[c, a], jm),
+            (snd2.at[c, lo], r2a.at[c], jm),
+            (snd2.at[c, hi], r2b.at[c], jp),
+            (s_p.at[c, lo], r_m.at[c, lo], jp),
+            (s_m.at[c, hi], r_p.at[c, hi], jm),
+            (s_p.at[c, hi], r_m.at[c, hi], jp),
+            (s_m.at[c, lo], r_p.at[c, lo], jm),
         )[n]
-        return remote(src, dst, ys.at[c, n], yr.at[c, n], ydev(to))
-
-    def compute(c, slot):
+        return remote(src, dst, ys.at[b, n], yr.at[b, n], ydev(to))
+
+    def compute(b, slots):
+        c0, n = BLOCKS[b]
 
         def part(d):
             sl = pl.ds(pl.multiple_of(d * rows, rows), rows)
-            rhs0 = vb[c, 0].reshape(kdim, W)
-            rhs1 = vb[c, 1].reshape(kdim, W)
-            return (jnp.dot(lhs[sl, 0:kdim], rhs0, preferred_element_type=F32)
-                    + jnp.dot(lhs[sl, kdim:2 * kdim], rhs1, preferred_element_type=F32))
-
-        slot(0)
-        snd2[c] = part(jo).astype(BF16)
-        ycopy(c, 0).start()
-        ycopy(c, 1).start()
-        slot(1)
-        res = part(jp)
-        s_p[c, 0:half] = res[0:half].astype(BF16)
-        h_p[c % (LAG + 1)] = res[half:]
-        ycopy(c, 2).start()
-        slot(2)
-        res = part(jm)
-        s_m[c, half:rows] = res[half:].astype(BF16)
-        h_m[c % (LAG + 1)] = res[0:half]
-        ycopy(c, 3).start()
-        slot(3)
-        own[c % (LAG2 + 1)] = part(j)
-
-    def combine(c):
-        ycopy(c, 1).wait_recv()
-        s_p[c, half:rows] = (h_p[c % (LAG + 1)] + r2b[c].astype(F32)).astype(BF16)
-        ycopy(c, 4).start()
-        ycopy(c, 0).wait_recv()
-        s_m[c, 0:half] = (h_m[c % (LAG + 1)] + r2a[c].astype(F32)).astype(BF16)
-        ycopy(c, 5).start()
-
-    def final(c):
+            total = None
+            for t in range(2):
+                rhs = [vb[c, t].reshape(kdim, W) for c in range(c0, c0 + n)]
+                rhs = rhs[0] if n == 1 else jnp.concatenate(rhs, axis=1)
+                term = jnp.dot(lhs[sl, t * kdim:(t + 1) * kdim], rhs, preferred_element_type=F32)
+                total = term if total is None else total + term
+            return [total[:, i * W:(i + 1) * W] for i in range(n)]
+
+        stages(slots[0])
+        for i, res in enumerate(part(jo)):
+            snd2[c0 + i] = res.astype(BF16)
+        ycopy(b, 0).start()
+        ycopy(b, 1).start()
+        stages(slots[1])
+        for i, res in enumerate(part(jp)):
+            s_p[c0 + i, 0:half] = res[0:half].astype(BF16)
+            h_p[c0 + i] = res[half:]
+        ycopy(b, 2).start()
+        stages(slots[2])
+        for i, res in enumerate(part(jm)):
+            s_m[c0 + i, half:rows] = res[half:].astype(BF16)
+            h_m[c0 + i] = res[0:half]
+        ycopy(b, 3).start()
+        stages(slots[3])
+        for i, res in enumerate(part(j)):
+            own[c0 + i] = res
+
+    def block_chunks(b):
+        c0, n = BLOCKS[b]
+        return range(c0, c0 + n)
+
+    def combine(b):
+        ycopy(b, 1).wait_recv()
+        for c in block_chunks(b):
+            s_p[c, half:rows] = (h_p[c] + r2b[c].astype(F32)).astype(BF16)
+        ycopy(b, 4).start()
+        ycopy(b, 0).wait_recv()
+        for c in block_chunks(b):
+            s_m[c, 0:half] = (h_m[c] + r2a[c].astype(F32)).astype(BF16)
+        ycopy(b, 5).start()
+
+    def final(b):
         for n in (2, 3, 4, 5):
-            ycopy(c, n).wait_recv()
-        cols = pl.ds(pl.multiple_of(c * W, W), W)
-        total = own[c % (LAG2 + 1)] + r_p[c].astype(F32) + r_m[c].astype(F32)
-        out[:, cols] = (total / (ve[:, cols] - pb[...])).astype(BF16)
+            ycopy(b, n).wait_recv()
+        for c in block_chunks(b):
+            cols = slice(c * W, (c + 1) * W)
+            total = own[c] + r_p[c].astype(F32) + r_m[c].astype(F32)
+            out[:, cols] = (total / (ve[:, cols] - pb[...])).astype(BF16)
 
     own_copy.wait()
     stages(PRE[0])
@@ -401,29 +420,16 @@
         relayout(q)
         stages(PRE[q])
 
-    @pl.loop(0, chunks)
-    def _(c):
-        def slot(n):
-            for cc, slots in enumerate(PLAN):
-                if slots[n]:
-                    @pl.when(c == cc)
-                    def _():
-                        stages(slots[n])
-
-        compute(c, slot)
-
-        @pl.when(c >= LAG)
-        def _():
-            combine(c - LAG)
-
-        @pl.when(c >= LAG2)
-        def _():
-            final(c - LAG2)
-
-    for n in range(LAG, 0, -1):
-        combine(chunks - n)
-    for n in range(LAG2, 0, -1):
-        final(chunks - n)
+    for b in range(NB):
+        compute(b, PLAN[b])
+        if b >= LAG:
+            combine(b - LAG)
+        if b >= LAG2:
+            final(b - LAG2)
+    for b in range(NB - LAG, NB):
+        combine(b)
+    for b in range(NB - LAG2, NB):
+        final(b)
 
     for g in range(NG):
         for d in first_zd(g):
@@ -455,10 +461,9 @@
             for cp in cols_all(g) + [col_partner(g, d) for d in range(XN)]:
                 cp.wait_send()
 
-    @pl.loop(0, chunks)
-    def _(c):
+    for b in range(NB):
         for n in range(6):
-            ycopy(c, n).wait_send()
+            ycopy(b, n).wait_send()
 
 
 def on_device(amplitudes, tile_mask, integrals, pair_energy, virt_energy):
@@ -473,10 +478,13 @@
     dma = pltpu.SemaphoreType.DMA
     return pl.pallas_call(
         kernel,
-        out_shape=jax.ShapeDtypeStruct((rows, ab), BF16),
-        in_specs=[pl.BlockSpec(memory_space=pl.ANY), vmem, pl.BlockSpec(memory_space=pl.ANY), vmem, vmem],
+        out_shape=pltpu.VMEM((rows, ab), BF16),
+        in_specs=[pl.BlockSpec(memory_space=pltpu.HBM)] * 5,
         out_specs=vmem,
         scratch_shapes=[
+            pltpu.VMEM((tiles, pairs), jnp.int32),
+            pltpu.VMEM((1, rows), F32),
+            pltpu.VMEM((1, ab), F32),
             pltpu.VMEM(amp.shape, BF16),
             pltpu.VMEM((pairs, tiles * kdim), BF16),
             pltpu.VMEM((chunks, tiles, depth, W), BF16),
@@ -491,11 +499,12 @@
             pltpu.VMEM((chunks, half, W), BF16),
             pltpu.VMEM((chunks, rows, W), BF16),
             pltpu.VMEM((chunks, rows, W), BF16),
-            pltpu.VMEM((LAG + 1, half, W), F32),
-            pltpu.VMEM((LAG + 1, half, W), F32),
-            pltpu.VMEM((LAG2 + 1, rows, W), F32),
+            pltpu.VMEM((chunks, half, W), F32),
+            pltpu.VMEM((chunks, half, W), F32),
+            pltpu.VMEM((chunks, rows, W), F32),
             dma((4,)),
             dma((chunks,)),
+            dma((3,)),
             dma,
             dma((len(FIRST), ZN, KN)),
             dma((len(FIRST), ZN, KN)),
@@ -509,8 +518,8 @@
             dma((NG, 11)),
             dma((NG, ZN)),
             dma((NG, ZN)),
-            dma((chunks, 6)),
-            dma((chunks, 6)),
+            dma((NB, 6)),
+            dma((NB, 6)),
         ],
         compiler_params=pltpu.CompilerParams(collective_id=0, has_side_effects=True),
         name="ladder",

time: 56.6 us -> 52.5 us (0.928)
  Pallas kernels: 54.5 us -> 51.6 us
  local copies, waits for them, and re-layouts: 1.87 us -> 0.8 us
    pallas_call x1, Pallas kernels: 54.5 us -> 51.6 us  [on_device(): pl.pallas_call(kernel, out_shape=pltpu.VMEM((rows, ab), BF16), in_specs=[...]
    unnamed x1, local copies, waits for them, and re-layouts: 1.87 us -> 0.8 us
where the time goes in v4:
time: 52.5 us; the launch traced here: 52.4 us
  Pallas kernels  51.6 us (98%)
  local copies, waits for them, and re-layouts  0.8 us (2%)
    pallas_call x1, Pallas kernels, on_device(): pl.pallas_call(kernel, out_shape=pltpu.VMEM((rows, ab), BF16), in_specs=[...  51.6 us

profile of v4, /device:TPU:1, one launch (start us, length us, event | category | flops | bytes accessed | tf_op | source)
XLA Modules:
  0.0 52.4 jit_solution(17306532088396347148)
XLA Ops:
  0.0 51.6 %ladder.1 = bf16[256,1024]{1,0:T(8,128)(2,1)S(1)} custom-call(bf16[16384,128]{1,0:T(8,128)(2,1)} %bitcast.8, s32[2,1024]{1,0:T(2,128)} %bitcast.9, bf16[2,16,1024]{2,1,0:T(8,128)(2,1)} %vin.1, f32[1,256]{1,0:T(1,128)} %bitcast.11, f32[1,1024]{1,0:T(1,128)} %bitcast.10), custom_call_target="tpu_custom_call" | custom-call | tf_op jit(solution)/shard_map/ladder/pallas_call | solution.py:479
  51.6 0.8 %copy.8 = bf16[256,1024]{1,0:T(8,128)(2,1)} copy(bf16[256,1024]{1,0:T(8,128)(2,1)S(1)} %ladder.1) | data formatting | bytes 1048576

commit v5 on v4

--- a/solution.py
+++ b/solution.py
@@ -101,17 +101,6 @@
     own_copy = pltpu.make_async_copy(vt.at[:, k], vb.at[:, k, x, z, k], vsem)
     own_copy.start()
 
-    r = lax.broadcasted_iota(jnp.int32, (256, 256), 0)
-    s = lax.broadcasted_iota(jnp.int32, (256, 256), 1)
-    target = (r & 15) * 16 + ((r >> 4) & 7) * 2 + (r >> 7)
-    perm[...] = jnp.where(s == target, 1.0, 0.0).astype(BF16)
-    for cp in small:
-        cp.wait()
-    for t in range(2):
-        row = mask[t:t + 1, :].astype(F32)
-        mb[t] = jnp.broadcast_to(row, (128, pairs)).T
-    pb[...] = jnp.broadcast_to(pe[...], (128, rows)).T
-
     def relayout(q):
         amp_copy(q).wait()
         steps = part_rows // 512
@@ -130,7 +119,6 @@
                         lhs[pl.ds(p0, 16), pl.ds(t * kdim + kt * 128, 128)] = (
                             res[o:o + 16, b * 128:b * 128 + 128] * m).astype(BF16)
 
-    relayout(0)
     pl.semaphore_wait(barrier, len(friends))
 
     def gsl(g):
@@ -414,9 +402,19 @@
             total = own[c] + r_p[c].astype(F32) + r_m[c].astype(F32)
             out[:, cols] = (total / (ve[:, cols] - pb[...])).astype(BF16)
 
+    r = lax.broadcasted_iota(jnp.int32, (256, 256), 0)
+    s = lax.broadcasted_iota(jnp.int32, (256, 256), 1)
+    target = (r & 15) * 16 + ((r >> 4) & 7) * 2 + (r >> 7)
+    perm[...] = jnp.where(s == target, 1.0, 0.0).astype(BF16)
+    for cp in small:
+        cp.wait()
+    for t in range(2):
+        line = mask[t:t + 1, :].astype(F32)
+        mb[t] = jnp.broadcast_to(line, (128, pairs)).T
+    pb[...] = jnp.broadcast_to(pe[...], (128, rows)).T
+
     own_copy.wait()
-    stages(PRE[0])
-    for q in range(1, parts):
+    for q in range(parts):
         relayout(q)
         stages(PRE[q])
 

time: 52.5 us -> 51.9 us (0.989)
  Pallas kernels: 51.6 us -> 51 us
    pallas_call x1, Pallas kernels: 51.6 us -> 51 us  [on_device(): pl.pallas_call(kernel, out_shape=pltpu.VMEM((rows, ab), BF16), in_specs=[...]
where the time goes in v5:
time: 51.9 us; the launch traced here: 51.8 us
  Pallas kernels  51 us (98%)
  local copies, waits for them, and re-layouts  0.8 us (2%)
    pallas_call x1, Pallas kernels, on_device(): pl.pallas_call(kernel, out_shape=pltpu.VMEM((rows, ab), BF16), in_specs=[...  51 us

profile of v5, /device:TPU:1, one launch (start us, length us, event | category | flops | bytes accessed | tf_op | source)
XLA Modules:
  0.0 51.8 jit_solution(5971873549020283886)
XLA Ops:
  0.0 51.0 %ladder.1 = bf16[256,1024]{1,0:T(8,128)(2,1)S(1)} custom-call(bf16[16384,128]{1,0:T(8,128)(2,1)} %bitcast.8, s32[2,1024]{1,0:T(2,128)} %bitcast.9, bf16[2,16,1024]{2,1,0:T(8,128)(2,1)} %vin.1, f32[1,256]{1,0:T(1,128)} %bitcast.11, f32[1,1024]{1,0:T(1,128)} %bitcast.10), custom_call_target="tpu_custom_call" | custom-call | tf_op jit(solution)/shard_map/ladder/pallas_call | solution.py:477
  51.0 0.8 %copy.8 = bf16[256,1024]{1,0:T(8,128)(2,1)} copy(bf16[256,1024]{1,0:T(8,128)(2,1)S(1)} %ladder.1) | data formatting | bytes 1048576

commit v6 on v5

--- a/solution.py
+++ b/solution.py
@@ -23,9 +23,9 @@
 )
 BLOCKS = ((0, 1), (1, 1), (2, 1), (3, 2), (5, 2), (7, 1))
 PLAN = (
-    ((('P', 0, 3),), (('P', 1, 2),), (), (('Q', 0, 3),)),
-    ((('Q', 1, 3), ('P', 1, 3)), (('P', 2, 2),), (), ()),
-    ((('P', 2, 3),), (('Q', 0, 4), ('Q', 1, 4)), (), ()),
+    ((('P', 0, 3),), (('P', 1, 2),), (('Q', 0, 3),), ()),
+    ((('Q', 1, 3), ('P', 1, 3)), (('P', 2, 2),), (), (('Q', 0, 4),)),
+    ((('P', 2, 3),), (('Q', 1, 4),), (), ()),
     ((('Q', 0, 5), ('Q', 0, 6)), (), (), (('Q', 1, 5),)),
     ((('Q', 1, 6),), (), (), ()),
     ((), (), (), ()),

time: 51.9 us -> 51.4 us (level)
  Pallas kernels: 51 us -> 50.3 us
    pallas_call x1, Pallas kernels: 51 us -> 50.3 us  [on_device(): pl.pallas_call(kernel, out_shape=pltpu.VMEM((rows, ab), BF16), in_specs=[...]
where the time goes in v6:
time: 51.4 us; the launch traced here: 51.1 us
  Pallas kernels  50.3 us (98%)
  local copies, waits for them, and re-layouts  0.8 us (2%)
    pallas_call x1, Pallas kernels, on_device(): pl.pallas_call(kernel, out_shape=pltpu.VMEM((rows, ab), BF16), in_specs=[...  50.3 us

profile of v6, /device:TPU:1, one launch (start us, length us, event | category | flops | bytes accessed | tf_op | source)
XLA Modules:
  0.0 51.1 jit_solution(7846966632449114560)
XLA Ops:
  0.0 50.3 %ladder.1 = bf16[256,1024]{1,0:T(8,128)(2,1)S(1)} custom-call(bf16[16384,128]{1,0:T(8,128)(2,1)} %bitcast.8, s32[2,1024]{1,0:T(2,128)} %bitcast.9, bf16[2,16,1024]{2,1,0:T(8,128)(2,1)} %vin.1, f32[1,256]{1,0:T(1,128)} %bitcast.11, f32[1,1024]{1,0:T(1,128)} %bitcast.10), custom_call_target="tpu_custom_call" | custom-call | tf_op jit(solution)/shard_map/ladder/pallas_call | solution.py:477
  50.4 0.8 %copy.8 = bf16[256,1024]{1,0:T(8,128)(2,1)} copy(bf16[256,1024]{1,0:T(8,128)(2,1)S(1)} %ladder.1) | data formatting | bytes 1048576
